TPU v7x, 32 devices: a whole 2x2x4 slice. The times are simulated.
32 devices in a mesh: seq: 8 (over y, x, core), fsdp: 4 (over z).
Axes of the slice: x: 2, y: 2, z: 4, core: 2. Of those that a mesh axis runs over, the one named last changes fastest.
Arguments:
- hidden_in: bfloat16 [4, 2048, 1024], P('fsdp', 'seq'), may hold values from -6 to 6
- cotangent: bfloat16 [4, 2048, 1024], P('fsdp', 'seq'), may hold values from -6 to 6
- doc_position: int32 [4, 2048], P('fsdp', 'seq'), may hold values from 0 to 2047, as said below
- norm_gains: float32 [2, 1024], P(None, ('seq', 'fsdp')), may hold values from 0.5 to 1.5
- conv_taps: float32 [3, 1024], P(None, ('seq', 'fsdp')), may hold values from -3 to 3
- in_proj: float32 [1024, 3072], P(('seq', 'fsdp')), may hold values from -0.1875 to 0.1875
- out_proj: float32 [1024, 1024], P(('seq', 'fsdp')), may hold values from -0.1875 to 0.1875
- gate_up: float32 [1024, 9216], P(('seq', 'fsdp')), may hold values from -0.1875 to 0.1875
- down_proj: float32 [4608, 1024], P(('seq', 'fsdp')), may hold values from -0.09375 to 0.09375
- first_gains: float32 [2, 1024], P(None, ('seq', 'fsdp')), may hold values from -56 to 56
- first_taps: float32 [3, 1024], P(None, ('seq', 'fsdp')), may hold values from -56 to 56
- first_in: float32 [1024, 3072], P(('seq', 'fsdp')), may hold values from -56 to 56
- first_out: float32 [1024, 1024], P(('seq', 'fsdp')), may hold values from -56 to 56
- first_gate_up: float32 [1024, 9216], P(('seq', 'fsdp')), may hold values from -14 to 14
- first_down: float32 [4608, 1024], P(('seq', 'fsdp')), may hold values from -32 to 32
- second_gains: float32 [2, 1024], P(None, ('seq', 'fsdp')), may hold values from 2.4576 to 24.576
- second_taps: float32 [3, 1024], P(None, ('seq', 'fsdp')), may hold values from 2.4576 to 24.576
- second_in: float32 [1024, 3072], P(('seq', 'fsdp')), may hold values from 2.4576 to 24.576
- second_out: float32 [1024, 1024], P(('seq', 'fsdp')), may hold values from 2.4576 to 24.576
- second_gate_up: float32 [1024, 9216], P(('seq', 'fsdp')), may hold values from 0.16384 to 1.6384
- second_down: float32 [4608, 1024], P(('seq', 'fsdp')), may hold values from 0.8192 to 8.192
Outputs:
- block_out: float32 [4, 2048, 1024], P('fsdp', 'seq')
- grad_hidden: float32 [4, 2048, 1024], P('fsdp', 'seq')
- grad_gains: float32 [2, 1024], P(None, ('seq', 'fsdp'))
- grad_taps: float32 [3, 1024], P(None, ('seq', 'fsdp'))
- grad_in: float32 [1024, 3072], P(('seq', 'fsdp'))
- grad_out: float32 [1024, 1024], P(('seq', 'fsdp'))
- grad_gate_up: float32 [1024, 9216], P(('seq', 'fsdp'))
- grad_down: float32 [4608, 1024], P(('seq', 'fsdp'))
- new_gains: float32 [2, 1024], P(None, ('seq', 'fsdp'))
- new_taps: float32 [3, 1024], P(None, ('seq', 'fsdp'))
- new_in: float32 [1024, 3072], P(('seq', 'fsdp'))
- new_out: float32 [1024, 1024], P(('seq', 'fsdp'))
- new_gate_up: float32 [1024, 9216], P(('seq', 'fsdp'))
- new_down: float32 [4608, 1024], P(('seq', 'fsdp'))
- next_first_gains: float32 [2, 1024], P(None, ('seq', 'fsdp'))
- next_first_taps: float32 [3, 1024], P(None, ('seq', 'fsdp'))
- next_first_in: float32 [1024, 3072], P(('seq', 'fsdp'))
- next_first_out: float32 [1024, 1024], P(('seq', 'fsdp'))
- next_first_gate_up: float32 [1024, 9216], P(('seq', 'fsdp'))
- next_first_down: float32 [4608, 1024], P(('seq', 'fsdp'))
- next_second_gains: float32 [2, 1024], P(None, ('seq', 'fsdp'))
- next_second_taps: float32 [3, 1024], P(None, ('seq', 'fsdp'))
- next_second_in: float32 [1024, 3072], P(('seq', 'fsdp'))
- next_second_out: float32 [1024, 1024], P(('seq', 'fsdp'))
- next_second_gate_up: float32 [1024, 9216], P(('seq', 'fsdp'))
- next_second_down: float32 [4608, 1024], P(('seq', 'fsdp'))
Inputs may be any that keep to these rules, and one draw needn't show every extreme that they name: doc_position[s, t] is 0 where a packed document starts (always at t = 0) and doc_position[s, t - 1] + 1 elsewhere; sequence 0 holds a single document.
All inputs are finite; a program needn't handle non-finite values.
Results may differ from a plain program's by a relative error of at most 0.012.
The roundings to bfloat16 on the way count: a program that leaves them out, or rounds other values in their place, can miss the bound.
Values may be sent and summed in bfloat16 or wider, within the bound.
A program may use at most 256 MiB of HBM per device.

v0:
```python
import jax
import jax.numpy as jnp
from jax import lax
from jax.sharding import PartitionSpec as P

STEP = 3


NORM_EPS = 1e-05
BETA_ONE = 0.9
BETA_TWO = 0.999
ADAM_EPS = 1e-08
RATE_MATRIX = 0.005
RATE_VECTOR = 0.2
DECAY = 0.1


def from_behind(value, axis, steps):
    count = lax.axis_size(axis)
    first, last = (max(0, -steps), min(count, count - steps))
    return lax.ppermute(value, axis, [(source, source + steps) for source in range(first, last)])


def matmul(left, right):
    return jnp.dot(left, right, preferred_element_type=jnp.float32)


def matmul_tn(left, right):
    return lax.dot_general(
        left, right, (((0,), (0,)), ((), ())), preferred_element_type=jnp.float32
    )


def matmul_nt(left, right):
    return lax.dot_general(
        left, right, (((1,), (1,)), ((), ())), preferred_element_type=jnp.float32
    )


def inverse_rms(values):
    return lax.rsqrt(jnp.mean(values * values, axis=-1, keepdims=True) + NORM_EPS)


def norm_backward(values, scale, gain, grad_normed):
    weighted = grad_normed * gain
    grad_gain = jnp.sum(grad_normed * values * scale, axis=0)
    cubed = scale * scale * scale
    grad_values = scale * weighted - values * cubed * jnp.mean(
        weighted * values, axis=-1, keepdims=True
    )
    return (grad_values, grad_gain)


def adamw_update(param, grad, first, second, rate, decay):
    first_new = BETA_ONE * first + (1.0 - BETA_ONE) * grad
    second_new = BETA_TWO * second + (1.0 - BETA_TWO) * grad * grad
    first_hat = first_new / (1.0 - BETA_ONE**STEP)
    second_hat = second_new / (1.0 - BETA_TWO**STEP)
    param_new = param - rate * (first_hat / (jnp.sqrt(second_hat) + ADAM_EPS) + decay * param)
    return (param_new, first_new, second_new)


def local(
    hidden_in,
    cotangent,
    doc_position,
    norm_gains,
    conv_taps,
    in_proj,
    out_proj,
    gate_up,
    down_proj,
    first_gains,
    first_taps,
    first_in,
    first_out,
    first_gate_up,
    first_down,
    second_gains,
    second_taps,
    second_in,
    second_out,
    second_gate_up,
    second_down,
):
    half = jnp.bfloat16
    single = jnp.float32
    row_count, length, width = hidden_in.shape
    tok_count = row_count * length
    mixer_full = (
        lax.all_gather(norm_gains.astype(half), ("seq", "fsdp"), axis=1, tiled=True),
        lax.all_gather(conv_taps.astype(half), ("seq", "fsdp"), axis=1, tiled=True),
        lax.all_gather(in_proj.astype(half), ("seq", "fsdp"), axis=0, tiled=True),
        lax.all_gather(out_proj.astype(half), ("seq", "fsdp"), axis=0, tiled=True),
    )
    gains_f = mixer_full[0].astype(single)
    taps_f = mixer_full[1].astype(single)
    resid_one = hidden_in.reshape(tok_count, width).astype(single)
    scale_one = inverse_rms(resid_one)
    normed_one = (resid_one * scale_one * gains_f[0]).astype(half)
    projected = matmul(normed_one, mixer_full[2])
    b_branch = projected[:, :width]
    c_branch = projected[:, width : 2 * width]
    x_branch = projected[:, 2 * width :]
    gated_input = (b_branch * x_branch).astype(half)
    gated_rows = gated_input.reshape(row_count, length, width)
    carried = from_behind(gated_rows[:, length - 2 :, :], "seq", 1)
    extended = jnp.concatenate([carried, gated_rows], axis=1).astype(single)
    gated_f = extended[:, 2:].reshape(tok_count, width)
    prev_one = extended[:, 1 : length + 1].reshape(tok_count, width)
    prev_two = extended[:, :length].reshape(tok_count, width)
    positions = doc_position.reshape(tok_count)
    mask_one = (positions >= 1).astype(single)[:, None]
    mask_two = (positions >= 2).astype(single)[:, None]
    conv_out = (
        taps_f[0] * gated_f + mask_one * taps_f[1] * prev_one + mask_two * taps_f[2] * prev_two
    )
    mixer_act = (c_branch * conv_out).astype(half)
    resid_two = resid_one + matmul(mixer_act, mixer_full[3])
    scale_two = inverse_rms(resid_two)
    normed_two = (resid_two * scale_two * gains_f[1]).astype(half)
    ffn_full = (
        lax.all_gather(gate_up.astype(half), ("seq", "fsdp"), axis=0, tiled=True),
        lax.all_gather(down_proj.astype(half), ("seq", "fsdp"), axis=0, tiled=True),
    )
    hidden_units = ffn_full[0].shape[1] // 2
    ffn_pre = matmul(normed_two, ffn_full[0])
    gate_pre = ffn_pre[:, :hidden_units]
    up_pre = ffn_pre[:, hidden_units:]
    sigmoid_gate = jax.nn.sigmoid(gate_pre)
    silu_gate = gate_pre * sigmoid_gate
    ffn_act = (silu_gate * up_pre).astype(half)
    block_out = resid_two + matmul(ffn_act, ffn_full[1])
    cot_rows = cotangent.reshape(tok_count, width)
    grad_act = matmul_nt(cot_rows, ffn_full[1])
    grad_gate = grad_act * up_pre * sigmoid_gate * (1.0 + gate_pre * (1.0 - sigmoid_gate))
    grad_both = jnp.concatenate([grad_gate, grad_act * silu_gate], axis=1).astype(half)
    grad_normed = matmul_nt(grad_both, ffn_full[0])
    grad_down = matmul_tn(ffn_act, cot_rows)
    grad_gate_up = matmul_tn(normed_two, grad_both)
    ffn_grads = (
        lax.psum_scatter(grad_gate_up, ("seq", "fsdp"), scatter_dimension=0, tiled=True),
        lax.psum_scatter(grad_down, ("seq", "fsdp"), scatter_dimension=0, tiled=True),
    )
    norm_part, gain_two_grad = norm_backward(resid_two, scale_two, gains_f[1], grad_normed)
    grad_resid = cot_rows.astype(single) + norm_part
    resid_cast = grad_resid.astype(half)
    grad_mixer = matmul_nt(resid_cast, mixer_full[3])
    grad_cbranch = grad_mixer * conv_out
    grad_conv = grad_mixer * c_branch
    masked_one = mask_one * grad_conv
    masked_two = mask_two * grad_conv
    grad_taps = jnp.stack(
        [
            jnp.sum(grad_conv * gated_f, axis=0),
            jnp.sum(masked_one * prev_one, axis=0),
            jnp.sum(masked_two * prev_two, axis=0),
        ]
    )
    one_rows = masked_one.reshape(row_count, length, width)
    two_rows = masked_two.reshape(row_count, length, width)
    leading = from_behind((one_rows[:, :2, :], two_rows[:, :2, :]), "seq", -1)
    ext_one = jnp.concatenate([one_rows, leading[0]], axis=1)
    ext_two = jnp.concatenate([two_rows, leading[1]], axis=1)
    next_one = ext_one[:, 1 : length + 1].reshape(tok_count, width)
    next_two = ext_two[:, 2 : length + 2].reshape(tok_count, width)
    grad_gated = taps_f[0] * grad_conv + taps_f[1] * next_one + taps_f[2] * next_two
    grad_proj = jnp.concatenate(
        [grad_gated * x_branch, grad_cbranch, grad_gated * b_branch], axis=1
    ).astype(half)
    grad_normone = matmul_nt(grad_proj, mixer_full[2])
    first_part, gain_one_grad = norm_backward(resid_one, scale_one, gains_f[0], grad_normone)
    grad_hidden = grad_resid + first_part
    grad_gains = jnp.stack([gain_one_grad, gain_two_grad])
    grad_in = matmul_tn(normed_one, grad_proj)
    grad_out = matmul_tn(mixer_act, resid_cast)
    mixer_grads = (
        lax.psum_scatter(grad_gains, ("seq", "fsdp"), scatter_dimension=1, tiled=True),
        lax.psum_scatter(grad_taps, ("seq", "fsdp"), scatter_dimension=1, tiled=True),
        lax.psum_scatter(grad_in, ("seq", "fsdp"), scatter_dimension=0, tiled=True),
        lax.psum_scatter(grad_out, ("seq", "fsdp"), scatter_dimension=0, tiled=True),
    )
    owned = (
        mixer_grads[0],
        mixer_grads[1],
        mixer_grads[2],
        mixer_grads[3],
        ffn_grads[0],
        ffn_grads[1],
    )
    params = (norm_gains, conv_taps, in_proj, out_proj, gate_up, down_proj)
    firsts = (first_gains, first_taps, first_in, first_out, first_gate_up, first_down)
    seconds = (second_gains, second_taps, second_in, second_out, second_gate_up, second_down)
    rates = (RATE_VECTOR, RATE_VECTOR, RATE_MATRIX, RATE_MATRIX, RATE_MATRIX, RATE_MATRIX)
    decays = (0.0, 0.0, DECAY, DECAY, DECAY, DECAY)
    updated = [
        adamw_update(
            params[index], owned[index], firsts[index], seconds[index], rates[index], decays[index]
        )
        for index in range(6)
    ]
    out_rows = block_out.reshape(row_count, length, width)
    grad_rows = grad_hidden.reshape(row_count, length, width)
    return (
        out_rows,
        grad_rows,
        owned[0],
        owned[1],
        owned[2],
        owned[3],
        owned[4],
        owned[5],
        updated[0][0],
        updated[1][0],
        updated[2][0],
        updated[3][0],
        updated[4][0],
        updated[5][0],
        updated[0][1],
        updated[1][1],
        updated[2][1],
        updated[3][1],
        updated[4][1],
        updated[5][1],
        updated[0][2],
        updated[1][2],
        updated[2][2],
        updated[3][2],
        updated[4][2],
        updated[5][2],
    )


def solution(mesh):
    in_specs = (
        P("fsdp", "seq", None),
        P("fsdp", "seq", None),
        P("fsdp", "seq"),
        P(None, ("seq", "fsdp")),
        P(None, ("seq", "fsdp")),
        P(("seq", "fsdp"), None),
        P(("seq", "fsdp"), None),
        P(("seq", "fsdp"), None),
        P(("seq", "fsdp"), None),
        P(None, ("seq", "fsdp")),
        P(None, ("seq", "fsdp")),
        P(("seq", "fsdp"), None),
        P(("seq", "fsdp"), None),
        P(("seq", "fsdp"), None),
        P(("seq", "fsdp"), None),
        P(None, ("seq", "fsdp")),
        P(None, ("seq", "fsdp")),
        P(("seq", "fsdp"), None),
        P(("seq", "fsdp"), None),
        P(("seq", "fsdp"), None),
        P(("seq", "fsdp"), None),
    )
    out_specs = (
        P("fsdp", "seq", None),
        P("fsdp", "seq", None),
        P(None, ("seq", "fsdp")),
        P(None, ("seq", "fsdp")),
        P(("seq", "fsdp"), None),
        P(("seq", "fsdp"), None),
        P(("seq", "fsdp"), None),
        P(("seq", "fsdp"), None),
        P(None, ("seq", "fsdp")),
        P(None, ("seq", "fsdp")),
        P(("seq", "fsdp"), None),
        P(("seq", "fsdp"), None),
        P(("seq", "fsdp"), None),
        P(("seq", "fsdp"), None),
        P(None, ("seq", "fsdp")),
        P(None, ("seq", "fsdp")),
        P(("seq", "fsdp"), None),
        P(("seq", "fsdp"), None),
        P(("seq", "fsdp"), None),
        P(("seq", "fsdp"), None),
        P(None, ("seq", "fsdp")),
        P(None, ("seq", "fsdp")),
        P(("seq", "fsdp"), None),
        P(("seq", "fsdp"), None),
        P(("seq", "fsdp"), None),
        P(("seq", "fsdp"), None),
    )
    return jax.shard_map(local, mesh=mesh, in_specs=in_specs, out_specs=out_specs, check_vma=False)
```

profile of v0, /device:TPU:0, one launch (start us, length us, event | category | flops | bytes accessed | tf_op | source)
XLA Modules:
  0.0 1544.5 jit_solution(2354420414054643888)
XLA Ops:
  7.3 1.8 convert_element_type.89
  9.1 1.5 convert_element_type.99
  10.8 2.1 convert_element_type.101
  13.8 70.3 %all-gather = bf16[32,32,2]{1,2,0:T(2,128)(2,1)S(1)} all-gather(bf16[1,32,2]{1,2,0:T(2,128)(2,1)S(1)} %convert_bitcast_fusion.1), channel_id=1, replica_groups=mesh['seq'=8,'fsdp'=4] {'seq','fsdp'}, dimensions={0}, use_global_device_ids=true | all-gather | bytes 4224 | tf_op jit(solution)/shard_map/all_gather | solution.py:91
  84.3 63.6 %all-gather.1 = bf16[32,32,3]{1,2,0:T(4,128)(2,1)S(1)} all-gather(bf16[1,32,3]{1,2,0:T(4,128)(2,1)S(1)} %convert_bitcast_fusion), channel_id=1, replica_groups=mesh['seq'=8,'fsdp'=4] {'seq','fsdp'}, dimensions={0}, use_global_device_ids=true | all-gather | bytes 6336 | tf_op jit(solution)/shard_map/all_gather | solution.py:92
  148.2 4.7 fusion.35
  156.8 2.6 multiply_reduce_fusion.5
  159.4 108.8 %all-gather.11.cloned.1.call-done = bf16[1024,9216]{1,0:T(8,128)(2,1)} async-done(((bf16[32,9216]{1,0:T(8,128)(2,1)}), bf16[1024,9216]{1,0:T(8,128)(2,1)}) %all-gather.11.cloned.1.call-update) | async-done | bytes 18874384 | tf_op jit(solution)/shard_map/all_gather | solution.py:123
  268.3 13.9 fusion.44
  282.2 69.1 %all-gather.13.cloned.1.call-done = bf16[4608,1024]{1,0:T(8,128)(2,1)} async-done(((bf16[144,1024]{1,0:T(8,128)(2,1)}), bf16[4608,1024]{1,0:T(8,128)(2,1)}) %all-gather.13.cloned.1.call-update) | async-done | bytes 9437200 | tf_op jit(solution)/shard_map/all_gather | solution.py:124
  351.3 10.3 multiply_convert_fusion.1
  361.6 11.5 multiply_reduce_fusion.3
  373.0 1.8 subtract_add_fusion
  375.9 2.5 multiply_reduce_fusion.2
  385.9 2.7 multiply_convert_fusion.5
  388.6 1.6 multiply_convert_fusion.3
  390.2 5.9 fusion.14
  397.2 2.7 fusion.30
  401.0 7.6 fusion.21
  409.7 9.6 fusion.25
  419.6 17.3 %fusion.1 = f32[1024,9216]{1,0:T(8,128)} fusion(bf16[256,4608]{1,0:T(8,128)(2,1)} %get-tuple-element.57, bf16[256,4608]{1,0:T(8,128)(2,1)} %copy-done.11, f32[256,1024]{1,0:T(8,128)S(1)} %get-tuple-element.74, f32[1024]{0:T(1024)S(1)} %bitcast.112, f32[256]{0:T(256)S(1)} %get-tuple-element.70), kind=kOutput, calls=%fused_computation.6 | convolution fusion | flops 4842061824 | bytes 43521024 | tf_op jit(solution)/shard_map/dot_general | solution.py:29
  437.0 8.1 fusion.3
  446.4 75.4 %reduce-scatter.21.cloned.1.call-done = f32[32,3]{1,0:T(8,128)} async-done(((f32[1024,3]{1,0:T(8,128)}), f32[32,3]{1,0:T(8,128)}) %reduce-scatter.21.cloned.1.call-update) | async-done | bytes 400
  522.7 134.5 %reduce-scatter.19.cloned.1.call-done = f32[32,2]{1,0:T(8,128)} async-done(((f32[1024,2]{1,0:T(8,128)}), f32[32,2]{1,0:T(8,128)}) %reduce-scatter.19.cloned.1.call-update) | async-done | bytes 272
  659.2 147.0 %reduce-scatter.13.cloned.1.call-done = f32[32,1024]{1,0:T(8,128)} async-done(((f32[1024,1024]{1,0:T(8,128)}), f32[32,1024]{1,0:T(8,128)}) %reduce-scatter.13.cloned.1.call-update) | async-done | bytes 131088 | tf_op jit(solution)/shard_map/reduce_scatter | solution.py:181
  806.1 1.7 multiply_subtract_fusion.3
  807.9 158.2 %reduce-scatter.11.cloned.1.call-done = f32[32,3072]{1,0:T(8,128)} async-done(((f32[1024,3072]{1,0:T(8,128)}), f32[32,3072]{1,0:T(8,128)}) %reduce-scatter.11.cloned.1.call-update) | async-done | bytes 393232 | tf_op jit(solution)/shard_map/reduce_scatter | solution.py:180
  966.0 2.4 multiply_subtract_fusion.2
  968.4 210.3 %reduce-scatter.17.cloned.1.call-done = f32[144,1024]{1,0:T(8,128)} async-done(((f32[4608,1024]{1,0:T(8,128)}), f32[144,1024]{1,0:T(8,128)}) %reduce-scatter.17.cloned.1.call-update) | async-done | bytes 589840 | tf_op jit(solution)/shard_map/reduce_scatter | solution.py:143
  1178.8 3.0 multiply_subtract_fusion.1
  1181.7 351.9 %reduce-scatter.15.cloned.1.call-done = f32[32,9216]{1,0:T(8,128)} async-done(((f32[1024,9216]{1,0:T(8,128)}), f32[32,9216]{1,0:T(8,128)}) %reduce-scatter.15.cloned.1.call-update) | async-done | bytes 1179664 | tf_op jit(solution)/shard_map/reduce_scatter | solution.py:142
  1533.7 4.0 multiply_subtract_fusion
  (128 shorter events, 21.4 us)
Async XLA Ops:
  7.2 77.0 %copy-start.26 = (f32[3,32]{1,0:T(4,128)S(1)}, f32[3,32]{1,0:T(4,128)}, u32[]{:S(2)}) copy-start(f32[3,32]{1,0:T(4,128)} %param.25) | copy-start | bytes 1156
  7.2 140.7 %copy-start.3 = (bf16[1,256,1024]{2,1,0:T(8,128)(2,1)S(1)}, bf16[1,256,1024]{2,1,0:T(8,128)(2,1)}, u32[]{:S(2)}) copy-start(bf16[1,256,1024]{2,1,0:T(8,128)(2,1)} %param.21) | copy-start | bytes 1572868
  7.2 141.0 %all-gather.7.cloned.1.call-start = ((), (), s32[]{:S(2)}) async-start(), calls=%async_computation.6 | async-start | bytes 6488064 | tf_op jit(solution)/shard_map/all_gather | solution.py:93
  9.1 147.8 %all-gather.9.cloned.1.call-start = ((), (), s32[]{:S(2)}) async-start(), calls=%async_computation.7 | async-start | bytes 2162688 | tf_op jit(solution)/shard_map/all_gather | solution.py:94
  10.7 257.6 %all-gather.11.cloned.1.call-start = ((), (), s32[]{:S(2)}) async-start(), calls=%async_computation.8 | async-start | bytes 19464192 | tf_op jit(solution)/shard_map/all_gather | solution.py:123
  12.9 338.3 %all-gather.13.cloned.1.call-start = ((), (), s32[]{:S(2)}) async-start(), calls=%async_computation.9 | async-start | bytes 9732096 | tf_op jit(solution)/shard_map/all_gather | solution.py:124
  13.8 508.1 %reduce-scatter.21.cloned.1.call-start = ((), (), s32[]{:S(2)}) async-start(), calls=%async_computation.15 | async-start | bytes 540672
  153.1 2.1 collective-permute-start
  156.8 125.4 %copy-start.6 = (bf16[256,1024]{1,0:T(8,128)(2,1)}, bf16[256,1024]{1,0:T(8,128)(2,1)S(1)}, u32[]{:S(2)}) copy-start(bf16[256,1024]{1,0:T(8,128)(2,1)S(1)} %get-tuple-element.54) | copy-start | bytes 1572868
  361.6 11.5 copy-start.11
  380.9 4.0 collective-permute-start.2
  382.2 3.7 collective-permute-start.1
  384.6 272.6 %reduce-scatter.19.cloned.1.call-start = ((), (), s32[]{:S(2)}) async-start(), calls=%async_computation.14 | async-start | bytes 540672
  388.6 7.5 copy-start.16
  397.2 408.9 %reduce-scatter.13.cloned.1.call-start = ((), (), s32[]{:S(2)}) async-start(), calls=%async_computation.11 | async-start | bytes 4325376 | tf_op jit(solution)/shard_map/reduce_scatter | solution.py:181
  400.0 566.0 %reduce-scatter.11.cloned.1.call-start = ((), (), s32[]{:S(2)}) async-start(), calls=%async_computation.10 | async-start | bytes 12976128 | tf_op jit(solution)/shard_map/reduce_scatter | solution.py:180
  408.7 770.1 %reduce-scatter.17.cloned.1.call-start = ((), (), s32[]{:S(2)}) async-start(), calls=%async_computation.13 | async-start | bytes 19464192 | tf_op jit(solution)/shard_map/reduce_scatter | solution.py:143
  419.3 1114.3 %reduce-scatter.15.cloned.1.call-start = ((), (), s32[]{:S(2)}) async-start(), calls=%async_computation.12 | async-start | bytes 38928384 | tf_op jit(solution)/shard_map/reduce_scatter | solution.py:142
  437.0 8.2 copy-start.21
  445.1 212.9 %copy-start.32 = (f32[2,32]{1,0:T(2,128)S(1)}, f32[2,32]{1,0:T(2,128)}, u32[]{:S(2)}) copy-start(f32[2,32]{1,0:T(2,128)} %param.30) | copy-start | bytes 772
  445.1 212.9 %copy-start.33 = (f32[2,32]{1,0:T(2,128)S(1)}, f32[2,32]{1,0:T(2,128)}, u32[]{:S(2)}) copy-start(f32[2,32]{1,0:T(2,128)} %param.36) | copy-start | bytes 772
  445.1 213.5 %copy-start.28 = (f32[3,32]{1,0:T(4,128)S(1)}, f32[3,32]{1,0:T(4,128)}, u32[]{:S(2)}) copy-start(f32[3,32]{1,0:T(4,128)} %param.31) | copy-start | bytes 1156
  445.1 213.5 %copy-start.29 = (f32[3,32]{1,0:T(4,128)S(1)}, f32[3,32]{1,0:T(4,128)}, u32[]{:S(2)}) copy-start(f32[3,32]{1,0:T(4,128)} %param.37) | copy-start | bytes 1156
  445.1 361.1 %copy-start.22 = (f32[32,1024]{1,0:T(8,128)S(1)}, f32[32,1024]{1,0:T(8,128)}, u32[]{:S(2)}) copy-start(f32[32,1024]{1,0:T(8,128)} %param.27) | copy-start | bytes 393220
  445.1 361.1 %copy-start.23 = (f32[32,1024]{1,0:T(8,128)S(1)}, f32[32,1024]{1,0:T(8,128)}, u32[]{:S(2)}) copy-start(f32[32,1024]{1,0:T(8,128)} %param.33) | copy-start | bytes 393220
  445.1 361.1 %copy-start.24 = (f32[32,1024]{1,0:T(8,128)S(1)}, f32[32,1024]{1,0:T(8,128)}, u32[]{:S(2)}) copy-start(f32[32,1024]{1,0:T(8,128)} %param.39) | copy-start | bytes 393220
  445.1 520.9 %copy-start.19 = (f32[32,3072]{1,0:T(8,128)S(1)}, f32[32,3072]{1,0:T(8,128)}, u32[]{:S(2)}) copy-start(f32[32,3072]{1,0:T(8,128)} %param.26) | copy-start | bytes 1179652
  445.1 733.6 %copy-start.13 = (f32[144,1024]{1,0:T(8,128)S(1)}, f32[144,1024]{1,0:T(8,128)}, u32[]{:S(2)}) copy-start(f32[144,1024]{1,0:T(8,128)} %param.29) | copy-start | bytes 1769476
  522.7 659.1 %copy-start.25 = (f32[3,32]{1,0:T(4,128)}, f32[3,32]{1,0:T(4,128)S(1)}, u32[]{:S(2)}) copy-start(f32[3,32]{1,0:T(4,128)S(1)} %copy.56) | copy-start | bytes 1156
  658.0 523.8 %copy-start.27 = (f32[2,32]{1,0:T(2,128)}, f32[2,32]{1,0:T(2,128)S(1)}, u32[]{:S(2)}) copy-start(f32[2,32]{1,0:T(2,128)S(1)} %copy.54) | copy-start | bytes 772
  807.8 725.8 %copy-start.5 = (f32[32,9216]{1,0:T(8,128)S(1)}, f32[32,9216]{1,0:T(8,128)}, u32[]{:S(2)}) copy-start(f32[32,9216]{1,0:T(8,128)} %param.28) | copy-start | bytes 3538948
  807.8 725.8 %copy-start.20 = (f32[32,9216]{1,0:T(8,128)S(1)}, f32[32,9216]{1,0:T(8,128)}, u32[]{:S(2)}) copy-start(f32[32,9216]{1,0:T(8,128)} %param.34) | copy-start | bytes 3538948
  (15 other events, 55.3 us)
Sparse Core Ops, SparseCore 0:
  11.5 72.0 all-gather.6
  87.1 54.9 all-gather.8
  145.4 122.7 all-gather.10
  271.5 79.7 all-gather.12
  384.7 137.1 reduce-scatter.20
  524.5 132.5 reduce-scatter.18
  660.0 146.0 reduce-scatter.12
  812.7 153.2 reduce-scatter.10
  973.0 205.7 reduce-scatter.16
  1185.6 347.9 reduce-scatter.14
where the time goes:
time: 1550 us; the launch traced here: 1540 us
  waiting for transfers between devices  1260 us (81%)
  blocking collectives  134 us (9%)
  matrix products  95 us (6%)
  other arithmetic  30.6 us (2%)
    reduce_scatter x1, waiting for transfers between devices, local(): lax.psum_scatter(grad_gate_up, ('seq', 'fsdp'), scatter_dimension=0, tile...  352 us
    reduce_scatter x1, waiting for transfers between devices, local(): lax.psum_scatter(grad_down, ('seq', 'fsdp'), scatter_dimension=0, tiled=T...  210 us
    unnamed x12, waiting for transfers between devices  210 us
    reduce_scatter x1, waiting for transfers between devices, local(): lax.psum_scatter(grad_in, ('seq', 'fsdp'), scatter_dimension=0, tiled=True)  158 us
    reduce_scatter x1, waiting for transfers between devices, local(): lax.psum_scatter(grad_out, ('seq', 'fsdp'), scatter_dimension=0, tiled=True)  147 us
    all_gather x1, waiting for transfers between devices, local(): lax.all_gather(gate_up.astype(half), ('seq', 'fsdp'), axis=0, tiled=True)  109 us
    all_gather x1, blocking collectives, local(): lax.all_gather(norm_gains.astype(half), ('seq', 'fsdp'), axis=1, tiled=True)  70.3 us
    all_gather x1, waiting for transfers between devices, local(): lax.all_gather(down_proj.astype(half), ('seq', 'fsdp'), axis=0, tiled=True)  69.1 us
  transfers between devices with their start and end apart: 13, of which 10 were waited for; matrix products, arithmetic and copies ran while one was open for 6% of the time, Pallas kernels for 0%

commit v1 on v0

--- a/solution.py
+++ b/solution.py
@@ -13,6 +13,7 @@
 RATE_MATRIX = 0.005
 RATE_VECTOR = 0.2
 DECAY = 0.1
+LANES = 128
 
 
 def from_behind(value, axis, steps):
@@ -87,14 +88,25 @@
     single = jnp.float32
     row_count, length, width = hidden_in.shape
     tok_count = row_count * length
-    mixer_full = (
-        lax.all_gather(norm_gains.astype(half), ("seq", "fsdp"), axis=1, tiled=True),
-        lax.all_gather(conv_taps.astype(half), ("seq", "fsdp"), axis=1, tiled=True),
-        lax.all_gather(in_proj.astype(half), ("seq", "fsdp"), axis=0, tiled=True),
-        lax.all_gather(out_proj.astype(half), ("seq", "fsdp"), axis=0, tiled=True),
-    )
-    gains_f = mixer_full[0].astype(single)
-    taps_f = mixer_full[1].astype(single)
+    axes = ("seq", "fsdp")
+    in_width = in_proj.shape[1]
+    out_width = out_proj.shape[1]
+    vectors = jnp.concatenate([norm_gains, conv_taps], axis=0).T.astype(half)
+    packed = jnp.concatenate(
+        [
+            in_proj.astype(half),
+            out_proj.astype(half),
+            jnp.pad(vectors, ((0, 0), (0, LANES - vectors.shape[1]))),
+        ],
+        axis=1,
+    )
+    packed_full = lax.all_gather(packed, axes, axis=0, tiled=True)
+    in_full = packed_full[:, :in_width]
+    out_full = packed_full[:, in_width : in_width + out_width]
+    vectors_full = packed_full[:, in_width + out_width :].astype(single).T
+    mixer_full = (None, None, in_full, out_full)
+    gains_f = vectors_full[:2]
+    taps_f = vectors_full[2:5]
     resid_one = hidden_in.reshape(tok_count, width).astype(single)
     scale_one = inverse_rms(resid_one)
     normed_one = (resid_one * scale_one * gains_f[0]).astype(half)
@@ -138,10 +150,6 @@
     grad_normed = matmul_nt(grad_both, ffn_full[0])
     grad_down = matmul_tn(ffn_act, cot_rows)
     grad_gate_up = matmul_tn(normed_two, grad_both)
-    ffn_grads = (
-        lax.psum_scatter(grad_gate_up, ("seq", "fsdp"), scatter_dimension=0, tiled=True),
-        lax.psum_scatter(grad_down, ("seq", "fsdp"), scatter_dimension=0, tiled=True),
-    )
     norm_part, gain_two_grad = norm_backward(resid_two, scale_two, gains_f[1], grad_normed)
     grad_resid = cot_rows.astype(single) + norm_part
     resid_cast = grad_resid.astype(half)
@@ -174,19 +182,30 @@
     grad_gains = jnp.stack([gain_one_grad, gain_two_grad])
     grad_in = matmul_tn(normed_one, grad_proj)
     grad_out = matmul_tn(mixer_act, resid_cast)
-    mixer_grads = (
-        lax.psum_scatter(grad_gains, ("seq", "fsdp"), scatter_dimension=1, tiled=True),
-        lax.psum_scatter(grad_taps, ("seq", "fsdp"), scatter_dimension=1, tiled=True),
-        lax.psum_scatter(grad_in, ("seq", "fsdp"), scatter_dimension=0, tiled=True),
-        lax.psum_scatter(grad_out, ("seq", "fsdp"), scatter_dimension=0, tiled=True),
-    )
+    vector_grads = jnp.concatenate([grad_gains, grad_taps], axis=0)
+    vector_count = vector_grads.shape[0]
+    grad_sent = jnp.concatenate(
+        [
+            grad_gate_up.astype(half),
+            grad_down.astype(half).reshape(width, -1),
+            grad_in.astype(half),
+            grad_out.astype(half),
+            jnp.pad(vector_grads.T, ((0, 0), (0, LANES - vector_count))).astype(half),
+        ],
+        axis=1,
+    )
+    grad_owned = lax.psum_scatter(grad_sent, axes, scatter_dimension=0, tiled=True).astype(single)
+    ends = [grad_gate_up.shape[1]]
+    for columns in (grad_down.size // width, in_width, out_width):
+        ends.append(ends[-1] + columns)
+    vector_owned = grad_owned[:, ends[3] : ends[3] + vector_count].T
     owned = (
-        mixer_grads[0],
-        mixer_grads[1],
-        mixer_grads[2],
-        mixer_grads[3],
-        ffn_grads[0],
-        ffn_grads[1],
+        vector_owned[:2],
+        vector_owned[2:],
+        grad_owned[:, ends[1] : ends[2]],
+        grad_owned[:, ends[2] : ends[3]],
+        grad_owned[:, : ends[0]],
+        grad_owned[:, ends[0] : ends[1]].reshape(down_proj.shape),
     )
     params = (norm_gains, conv_taps, in_proj, out_proj, gate_up, down_proj)
     firsts = (first_gains, first_taps, first_in, first_out, first_gate_up, first_down)

time: 1550 us -> 817 us (0.53)
  waiting for transfers between devices: 1260 us -> 572 us
  blocking collectives: 134 us -> 0 us
  local copies, waits for them, and re-layouts: 8.42 us -> 88.8 us
  other arithmetic: 30.6 us -> 46.5 us
    reduce_scatter x4 -> x0, waiting for transfers between devices: 867 us -> none  [the longest x1 352 us: local(): lax.psum_scatter(grad_gate_up, ('seq', 'fsdp'), scatter_dimension=0, tile...]
    all_gather x2 -> x0, blocking collectives: 134 us -> none  [the longest x1 70.3 us: local(): lax.all_gather(norm_gains.astype(half), ('seq', 'fsdp'), axis=1, tiled=True)]
    unnamed x12 -> x5, waiting for transfers between devices: 210 us -> 314 us
    all_gather x2 -> x1, waiting for transfers between devices: 0.02 us -> 76.6 us  [local(): packed_full = lax.all_gather(packed, axes, axis=0, tiled=True)]
    unnamed x72 -> x104, local copies, waits for them, and re-layouts: 8.21 us -> 62.9 us
    reshape x0 -> x2, local copies, waits for them, and re-layouts: none -> 18.5 us  [the longest x1 17.5 us: local(): grad_down.astype(half).reshape(width, -1)]
  transfers between devices with their start and end apart: 13 -> 7, of which waited for: 10 -> 5; matrix products, arithmetic and copies ran while one was open for 6% -> 11% of each run, Pallas kernels for 0% -> 0%
where the time goes in v1:
time: 817 us; the launch traced here: 811 us
  waiting for transfers between devices  572 us (70%)
  local copies, waits for them, and re-layouts  88.8 us (11%)
  matrix products  84.8 us (10%)
  other arithmetic  46.5 us (6%)
  between operations  14.7 us (2%)
    unnamed x5, waiting for transfers between devices  314 us
    all_gather x1, waiting for transfers between devices, local(): lax.all_gather(gate_up.astype(half), ('seq', 'fsdp'), axis=0, tiled=True)  112 us
    all_gather x1, waiting for transfers between devices, local(): packed_full = lax.all_gather(packed, axes, axis=0, tiled=True)  76.6 us
    all_gather x1, waiting for transfers between devices, local(): lax.all_gather(down_proj.astype(half), ('seq', 'fsdp'), axis=0, tiled=True)  69 us
    unnamed x104, local copies, waits for them, and re-layouts  62.9 us
    dot_general x4, matrix products, matmul(): return jnp.dot(left, right, preferred_element_type=jnp.float32)  31.2 us
    dot_general x4, matrix products, matmul_nt(): lax.dot_general(left, right, (((1,), (1,)), ((), ())), preferred_element_...  30 us
    sub x6, other arithmetic, adamw_update(): param - rate * (first_hat / (jnp.sqrt(second_hat) + ADAM_EPS) + decay * p...  23.7 us
  transfers between devices with their start and end apart: 7, of which 5 were waited for; matrix products, arithmetic and copies ran while one was open for 11% of the time, Pallas kernels for 0%

profile of v1, /device:TPU:0, one launch (start us, length us, event | category | flops | bytes accessed | tf_op | source)
XLA Modules:
  0.0 811.5 jit_solution(17906408216686123920)
XLA Ops:
  15.8 76.6 %all-gather.4.cloned.1.call-done = bf16[1024,4224]{1,0:T(8,128)(2,1)} async-done(((bf16[32,4224]{1,0:T(8,128)(2,1)}), bf16[1024,4224]{1,0:T(8,128)(2,1)}) %all-gather.4.cloned.1.call-update) | async-done | bytes 8650768 | tf_op jit(solution)/shard_map/all_gather | solution.py:103
  94.7 4.7 fusion.2
  104.1 2.6 multiply_reduce_fusion.5
  106.7 111.6 %all-gather.6.cloned.1.call-done = bf16[1024,9216]{1,0:T(8,128)(2,1)} async-done(((bf16[32,9216]{1,0:T(8,128)(2,1)}), bf16[1024,9216]{1,0:T(8,128)(2,1)}) %all-gather.6.cloned.1.call-update) | async-done | bytes 18874384 | tf_op jit(solution)/shard_map/all_gather | solution.py:135
  218.4 14.1 %fusion.49 = f32[256,9216]{1,0:T(8,128)} fusion(bf16[1024,9216]{1,0:T(8,128)(2,1)} %all-gather.6.cloned.1.call-done, f32[256,1024]{1,0:T(8,128)S(1)} %get-tuple-element.232, f32[1024]{0:T(1024)S(1)} %get-tuple-element.189, f32[256]{0:T(256)S(1)} %get-tuple-element.228), kind=kOutput, calls=%fused_computation.122 | convolution fusion | flops 4832624640 | bytes 29365248 | tf_op jit(solution)/shard_map/dot_general | solution.py:26
  232.5 69.0 %all-gather.8.cloned.1.call-done = bf16[4608,1024]{1,0:T(8,128)(2,1)} async-done(((bf16[144,1024]{1,0:T(8,128)(2,1)}), bf16[4608,1024]{1,0:T(8,128)(2,1)}) %all-gather.8.cloned.1.call-update) | async-done | bytes 9437200 | tf_op jit(solution)/shard_map/all_gather | solution.py:136
  301.5 14.2 %multiply_convert_fusion.1 = (bf16[256,4608]{1,0:T(8,128)(2,1)}, bf16[256,4608]{1,0:T(8,128)(2,1)}, bf16[256,4608]{1,0:T(8,128)(2,1)}) fusion(f32[256,9216]{1,0:T(8,128)} %fusion.49, bf16[4608,1024]{1,0:T(8,128)(2,1)} %all-gather.8.cloned.1.call-done, bf16[1,256,1024]{2,1,0:T(8,128)(2,1)S(1)} %copy-done.14), kind=kOutput, calls=%fused_computation.13 | convolution fusion | flops 2433613824 | bytes 26476544 | tf_op jit(solution)/shard_map/dot_general | solution.py:36
  315.7 11.6 %convert_dynamic-update-slice_fusion = bf16[1024,18048]{1,0:T(8,128)(2,1)} fusion(bf16[256,4608]{1,0:T(8,128)(2,1)} %get-tuple-element.220, bf16[256,4608]{1,0:T(8,128)(2,1)} %get-tuple-element.219, f32[256,1024]{1,0:T(8,128)S(1)} %get-tuple-element.232, f32[1024]{0:T(1024)S(1)} %get-tuple-element.189, f32[256]{0:T(256)S(1)} %get-tuple-element.228), kind=kOutput, calls=%fused_computation | convolution fusion | flops 4851499008 | bytes 24646656 | tf_op jit(solution)/shard_map/dot_general | solution.py:30
  327.2 10.6 %multiply_reduce_fusion.3 = (bf16[1024]{0:T(1024)(128)(2,1)S(1)}, f32[256]{0:T(256)S(1)}, f32[256,1024]{1,0:T(8,128)S(1)}) fusion(f32[256,1024]{1,0:T(8,128)S(1)} %get-tuple-element.232, f32[256]{0:T(256)S(1)} %get-tuple-element.228, f32[1024]{0:T(1024)S(1)} %get-tuple-element.189, bf16[1024,9216]{1,0:T(8,128)(2,1)} %all-gather.6.cloned.1.call-done, ...), kind=kOutput, calls=%fused_computation.60 | convolution fusion | flops 4842847232 | bytes 25698304 | tf_op jit(solution)/shard_map/dot_general | solution.py:36
  340.6 2.7 multiply_reduce_fusion
  347.1 5.3 convolution_convert_fusion
  352.3 17.5 %reshape.194 = bf16[1024,4608]{1,0:T(8,128)(2,1)} reshape(bf16[4608,1024]{1,0:T(8,128)(2,1)} %convolution_convert_fusion) | data formatting | bytes 18874368 | tf_op jit(solution)/shard_map/reshape | solution.py:190
  369.8 8.0 constant_dynamic-update-slice_fusion
  381.7 4.6 convert_dynamic-update-slice_fusion.1
  388.4 2.9 fusion.24
  396.1 2.9 copy.208
  404.3 3.2 copy.205
  407.5 4.2 copy.206
  411.7 9.9 %fusion.14 = f32[1,256,1024]{2,1,0:T(8,128)} fusion(f32[256,1024]{1,0:T(8,128)S(1)} %copy-done.6, bf16[256,4608]{1,0:T(8,128)(2,1)} %get-tuple-element.221, bf16[4608,1024]{1,0:T(8,128)(2,1)} %all-gather.8.cloned.1.call-done), kind=kOutput, calls=%fused_computation.35 | convolution fusion | flops 2416181248 | bytes 13893632 | tf_op jit(solution)/shard_map/dot_general | solution.py:26
  422.9 313.8 %reduce-scatter.4.cloned.1.call-done = bf16[32,18048]{1,0:T(8,128)(2,1)} async-done(((bf16[1024,18048]{1,0:T(8,128)(2,1)}), bf16[32,18048]{1,0:T(8,128)(2,1)}) %reduce-scatter.4.cloned.1.call-update) | async-done | bytes 1155088
  736.7 4.9 copy.223
  741.6 3.6 convert_element_type.120
  746.7 2.9 slice.146
  750.7 2.6 copy.209
  754.1 3.8 copy.211
  759.6 5.2 multiply_subtract_fusion.1
  764.8 2.6 copy.212
  767.4 2.9 multiply_subtract_fusion.3
  772.1 12.9 %multiply_subtract_fusion = (f32[32,9216]{0,1:T(8,128)}, f32[32,9216]{0,1:T(8,128)}, f32[32,9216]{0,1:T(8,128)}) fusion(f32[32,9216]{0,1:T(8,128)} %copy.208, f32[32,18048]{0,1:T(8,128)} %copy-done.1, f32[32,9216]{0,1:T(8,128)} %copy.205, f32[32,9216]{0,1:T(8,128)} %copy.206), kind=kLoop, calls=%fused_computation.10 | loop fusion | flops 4423680 | bytes 8257536 | tf_op jit(solution)/shard_map/sub | solution.py:60
  785.0 3.8 copy.214
  792.0 3.8 copy.217
  797.9 3.8 copy.220
  (154 shorter events, 54.1 us)
Async XLA Ops:
  7.2 8.4 %copy-start.16 = (bf16[1,256,1024]{2,1,0:T(8,128)(2,1)S(1)}, bf16[1,256,1024]{2,1,0:T(8,128)(2,1)}, u32[]{:S(2)}) copy-start(bf16[1,256,1024]{2,1,0:T(8,128)(2,1)} %param.21) | copy-start | bytes 1572868
  7.2 85.2 %all-gather.4.cloned.1.call-start = ((), (), s32[]{:S(2)}) async-start(), calls=%async_computation.1 | async-start | bytes 8921088 | tf_op jit(solution)/shard_map/all_gather | solution.py:103
  11.5 206.9 %all-gather.6.cloned.1.call-start = ((), (), s32[]{:S(2)}) async-start(), calls=%async_computation.2 | async-start | bytes 19464192 | tf_op jit(solution)/shard_map/all_gather | solution.py:135
  13.7 287.8 %all-gather.8.cloned.1.call-start = ((), (), s32[]{:S(2)}) async-start(), calls=%async_computation.3 | async-start | bytes 9732096 | tf_op jit(solution)/shard_map/all_gather | solution.py:136
  15.6 721.1 %reduce-scatter.4.cloned.1.call-start = ((), (), s32[]{:S(2)}) async-start(), calls=%async_computation.4 | async-start | bytes 38117376
  94.7 7.0 copy-start.33
  99.5 3.0 collective-permute-start
  104.1 128.4 %copy-start.11 = (bf16[256,1024]{1,0:T(8,128)(2,1)}, bf16[256,1024]{1,0:T(8,128)(2,1)S(1)}, u32[]{:S(2)}) copy-start(bf16[256,1024]{1,0:T(8,128)(2,1)S(1)} %get-tuple-element.217) | copy-start | bytes 1572868
  106.7 231.2 %copy-start.5 = (f32[256,1024]{1,0:T(8,128)}, f32[256,1024]{1,0:T(8,128)S(1)}, u32[]{:S(2)}) copy-start(f32[256,1024]{1,0:T(8,128)S(1)} %get-tuple-element.232) | copy-start | bytes 3145732
  218.4 83.1 %copy-start.14 = (bf16[1,256,1024]{2,1,0:T(8,128)(2,1)S(1)}, bf16[1,256,1024]{2,1,0:T(8,128)(2,1)}, u32[]{:S(2)}) copy-start(bf16[1,256,1024]{2,1,0:T(8,128)(2,1)} %param.22) | copy-start | bytes 1572868
  327.2 10.6 %copy-start.15 = (bf16[1,256,1024]{2,1,0:T(8,128)(2,1)S(1)}, bf16[1,256,1024]{2,1,0:T(8,128)(2,1)}, u32[]{:S(2)}) copy-start(bf16[1,256,1024]{2,1,0:T(8,128)(2,1)} %param.22) | copy-start | bytes 1572868
  340.6 6.5 copy-start.8
  344.5 33.4 %collective-permute-start.2 = (f32[1,2,1024]{2,1,0:T(2,128)S(1)}, f32[1,2,1024]{2,1,0:T(2,128)S(1)}, u32[]{:S(2)}, u32[]{:S(2)}) collective-permute-start(f32[1,2,1024]{2,1,0:T(2,128)S(1)} %slice.142), channel_id=1, source_target_pairs={{4,0},{8,4},{12,8},{16,12},{20,16},{24,20},{28,24},{5,1},{9,5},{13... | collective-permute-start | bytes 24584 | tf_op jit(solution)/shard_map/ppermute | solution.py:22
  345.8 32.1 %collective-permute-start.1 = (f32[1,2,1024]{2,1,0:T(2,128)S(1)}, f32[1,2,1024]{2,1,0:T(2,128)S(1)}, u32[]{:S(2)}, u32[]{:S(2)}) collective-permute-start(f32[1,2,1024]{2,1,0:T(2,128)S(1)} %slice.141), channel_id=1, source_target_pairs={{4,0},{8,4},{12,8},{16,12},{20,16},{24,20},{28,24},{5,1},{9,5},{13... | collective-permute-start | bytes 24584 | tf_op jit(solution)/shard_map/ppermute | solution.py:22
  377.9 10.6 %slice-start = ((s8[8650752]{0:T(1024)(128)(4,1)}), s8[4194304]{0:T(1024)(128)(4,1)S(1)}, s32[]{:S(2)}) async-start(s8[8650752]{0:T(1024)(128)(4,1)} %bitcast.84), calls=%async_computation.5 | async-start | bytes 8388608
  380.1 8.3 %slice-start.1 = ((s8[8650752]{0:T(1024)(128)(4,1)}), s8[4194304]{0:T(1024)(128)(4,1)S(1)}, s32[]{:S(2)}) async-start(s8[8650752]{0:T(1024)(128)(4,1)} %bitcast.84), calls=%async_computation.6 | async-start | bytes 8388608
  381.7 6.7 slice-start.2
  396.1 6.2 copy-start.28
  396.1 7.2 copy-start.29
  404.3 7.4 copy-start.6
  411.7 9.9 %copy-start.18 = (bf16[1,256,1024]{2,1,0:T(8,128)(2,1)S(1)}, bf16[1,256,1024]{2,1,0:T(8,128)(2,1)}, u32[]{:S(2)}) copy-start(bf16[1,256,1024]{2,1,0:T(8,128)(2,1)} %param.21) | copy-start | bytes 1572868
  411.7 9.9 %copy-start.21 = (f32[256,1024]{1,0:T(8,128)S(1)}, f32[256,1024]{1,0:T(8,128)}, u32[]{:S(2)}) copy-start(f32[256,1024]{1,0:T(8,128)} %get-tuple-element.234) | copy-start | bytes 3145732
  790.1 7.0 copy-start.13
  795.8 5.9 copy-start.34
  795.8 5.9 copy-start.35
  795.8 5.9 copy-start.36
  795.8 6.5 copy-start.30
  795.8 6.5 copy-start.31
  795.9 6.5 copy-start.32
  795.9 7.1 copy-start.9
  795.9 7.1 copy-start.10
  797.1 5.9 copy-start.23
  (15 other events, 59.5 us)
Sparse Core Ops, SparseCore 0:
  11.6 80.7 all-gather.3
  95.8 122.5 all-gather.5
  221.8 79.7 all-gather.7
  392.6 344.0 reduce-scatter.3
